TPU v7x, 128 devices: a whole 4x4x4 slice. The times are simulated.
128 devices in a mesh: blk: 8 (over x_lo, y), grid: 16 (over x_hi, z, core).
Axes of the slice: x: 4 (x_hi: 2, x_lo: 2; x = x_hi * 2 + x_lo), y: 4, z: 4, core: 2. Of those that a mesh axis runs over, the one named last changes fastest.
Arguments:
- conn: int32 [2048, 9], P(('blk', 'grid')), may hold values from 0 to 2047, as said below
- extract: float32 [9, 9, 2048], P(None, None, ('blk', 'grid')), may hold values from 0.1 to 1
- points: float32 [3, 9, 2048], P(None, None, ('blk', 'grid')), as said below
Outputs:
- factor: float32 [1, 2048, 2, 1024], P(None, 'grid', None, 'blk')
Inputs may be any that keep to these rules, and one draw needn't show every extreme that they name: `conn`: element e = ix 32 + iy of the periodic 64 x 32 grid of elements names the functions ((ix + s) mod 64) * 32 + (iy + t) mod 32 for s, t in 0, 1, 2, each once, in an order that differs from element to element. The 9 points of element e = ix 32 + iy are the 3 x 3 Gauss points of the cell [ix / 64, (ix + 1) / 64] x [iy / 64, (iy + 1) / 64], each coordinate then moved by at most 3.5 / 64; points[2] is positive.
All inputs are finite; a program needn't handle non-finite values.
Results may differ from a plain program's by a relative error of at most 0.0003.
Values sent between devices are 32-bit elements; how exact they have to be, the bound alone decides.
A program may use at most 128 MiB of HBM per device.

v0:
```python
import math
import jax
import jax.numpy as jnp
from jax import lax
from jax.sharding import PartitionSpec as P

M = 2048
EX = 64
EY = 32
QP = 9
TB = 128
kernel_gain = 0.02
mass_shift = 0.05


def spread(array, axis, root):
    mine = lax.axis_index(axis) == root
    return lax.psum(jnp.where(mine, array, jnp.zeros_like(array)), axis)


def bernstein_table():
    spread_root = 0.5 * math.sqrt(0.6)
    gauss_nodes = [0.5 - spread_root, 0.5, 0.5 + spread_root]

    def bern_poly(which, where):
        return [(1.0 - where) ** 2, 2.0 * where * (1.0 - where), where * where][which]

    table_rows = []
    for i in range(3):
        for j in range(3):
            table_row = []
            for a in range(3):
                for b in range(3):
                    table_row.append(bern_poly(a, gauss_nodes[i]) * bern_poly(b, gauss_nodes[j]))
            table_rows.append(table_row)
    return jnp.asarray(table_rows, jnp.float32)


def torus_square(first_x, first_y, second_x, second_y):
    height = EY / EX
    gap_x = jnp.abs(first_x - second_x)
    gap_x = jnp.minimum(gap_x, jnp.abs(1.0 - gap_x))
    gap_y = jnp.abs(first_y - second_y)
    gap_y = jnp.minimum(gap_y, jnp.abs(height - gap_y))
    return gap_x * gap_x + gap_y * gap_y


def kernel_rows(test_x, test_y, trial_x, trial_y, trial_w):
    distance = torus_square(test_x[:, None], test_y[:, None], trial_x[None, :], trial_y[None, :])
    return kernel_gain * trial_w[None, :] * (1.0 + distance * (EX * EX / 4.0)) ** (-1.75)


def local_values(extract_cube):
    return jnp.einsum(
        "kb,abn->nka", bernstein_table(), extract_cube, precision=lax.Precision.HIGHEST
    )


def basis_rows(values, links):
    count = links.shape[0]
    slot = jnp.arange(count * QP, dtype=jnp.int32).reshape(count, QP)
    row_index = jnp.broadcast_to(slot[:, :, None], (count, QP, QP))
    col_index = jnp.broadcast_to(links[:, None, :], (count, QP, QP))
    return jnp.zeros((count * QP, M), jnp.float32).at[row_index, col_index].add(values)


def window_width():
    wide = 128 + 4 * EY
    return wide


def fold_window(potential_wide):
    extra = potential_wide.shape[1] - M
    return potential_wide[:, :M] + jnp.pad(potential_wide[:, M:], ((0, 0), (0, M - extra)))


def tile_target(links, grid_size, tile_rows):
    tile = links // TB
    return tile % grid_size * (tile_rows * TB) + tile // grid_size * TB + links % TB


def add_potential(state, piece, first_element, test_x, test_y):
    points_flat, extract_flat, links_flat = piece
    count = points_flat.shape[1]
    span = math.gcd(count, 128)
    width = window_width()
    window_iota = jnp.arange(width, dtype=jnp.int32)

    def step(index, inner):
        potential_wide, total = inner
        first = index * span
        part_points = lax.dynamic_slice_in_dim(points_flat, first, span, 1).reshape(3, QP, span)
        part_extract = lax.dynamic_slice_in_dim(extract_flat, first, span, 1).reshape(QP, QP, span)
        part_links = lax.dynamic_slice_in_dim(links_flat, first, span, 1).T
        kernel_block = kernel_rows(
            test_x,
            test_y,
            part_points[0].T.reshape(-1),
            part_points[1].T.reshape(-1),
            part_points[2].T.reshape(-1),
        )
        total = total + jnp.sum(kernel_block, axis=1)
        offset = (first_element + first) // EY * EY
        local = (part_links - offset) % M
        ones = (local[:, :, None] == window_iota[None, None, :]).astype(jnp.float32)
        trial_phi = jnp.einsum(
            "eka,eaw->ekw", local_values(part_extract), ones, precision=lax.Precision.HIGHEST
        ).reshape(span * QP, width)
        block = jnp.dot(
            kernel_block,
            trial_phi,
            precision=lax.Precision.HIGHEST,
            preferred_element_type=jnp.float32,
        )
        current = lax.dynamic_slice_in_dim(potential_wide, offset, width, 1)
        potential_wide = lax.dynamic_update_slice_in_dim(potential_wide, current + block, offset, 1)
        return (potential_wide, total)

    return lax.fori_loop(0, count // span, step, state)


def shards(conn, extract, points):
    count = conn.shape[0]
    rows = count * QP
    links_flat = conn.T
    extract_flat = extract.reshape(QP * QP, count)
    points_flat = points.reshape(3 * QP, count)
    own_x = points[0].T.reshape(-1)
    own_y = points[1].T.reshape(-1)
    own_w = points[2].T.reshape(-1)
    own_values = local_values(extract)
    test_phi = basis_rows(own_values, conn)
    width = window_width()
    start_state = (jnp.zeros((rows, M + width), jnp.float32), jnp.zeros((rows,), jnp.float32))
    grid_size = lax.axis_size("grid")
    blk_size = lax.axis_size("blk")
    grid_at = lax.axis_index("grid")
    blk_at = lax.axis_index("blk")
    tile_rows = M // (TB * grid_size)
    tile_cols = M // (TB * blk_size)
    band = tile_cols * TB
    potential_wide, total = add_potential(
        start_state,
        (
            lax.all_gather(points_flat, ("blk", "grid"), axis=1, tiled=True),
            lax.all_gather(extract_flat, ("blk", "grid"), axis=1, tiled=True),
            lax.all_gather(links_flat, ("blk", "grid"), axis=1, tiled=True),
        ),
        jnp.int32(0),
        own_x,
        own_y,
    )
    potential = fold_window(potential_wide)
    share = own_w[:, None] * ((mass_shift + total)[:, None] * test_phi - potential)
    own_contrib = jnp.einsum(
        "eka,ekm->eam", own_values, share.reshape(count, QP, M), precision=lax.Precision.HIGHEST
    )
    split_cols = (
        own_contrib.reshape(rows, tile_cols, blk_size, TB)
        .transpose(2, 0, 1, 3)
        .reshape(blk_size, rows, band)
    )
    targets = tile_target(conn.reshape(-1), grid_size, tile_rows)
    placed = (
        jnp.zeros((blk_size, grid_size * tile_rows * TB, band), jnp.float32)
        .at[:, targets]
        .add(split_cols)
    )
    term = placed.reshape(blk_size * grid_size, -1)
    stiff = lax.psum_scatter(term, ("blk", "grid"), scatter_dimension=0, tiled=True).reshape(
        tile_rows, TB, tile_cols, TB
    )
    column_tiles = stiff[:, :, 0, :]
    mine = spread(column_tiles, "blk", 0)
    panel_tiles = lax.all_gather(mine, "grid", axis=0, tiled=True)
    panel = panel_tiles.reshape(grid_size, tile_rows, TB, TB).transpose(1, 0, 2, 3).reshape(M, TB)
    head = panel[:TB]
    lower = jnp.linalg.cholesky(0.5 * (head + head.T))
    rest = lax.linalg.triangular_solve(
        lower, panel[TB:], left_side=False, lower=True, transpose_a=True
    )
    factor_cols = jnp.concatenate([lower, rest], axis=0)
    row_part = lax.dynamic_index_in_dim(
        factor_cols.reshape(tile_rows, grid_size, TB, TB), grid_at, 1, keepdims=False
    )
    col_part = lax.dynamic_index_in_dim(
        factor_cols.reshape(tile_cols, blk_size, TB, TB), blk_at, 1, keepdims=False
    )
    update = jnp.einsum("xuw,yvw->xuyv", row_part, col_part, precision=lax.Precision.HIGHEST)
    tile_row = (jnp.arange(tile_rows, dtype=jnp.int32) * grid_size + grid_at)[:, None, None, None]
    tile_col = (jnp.arange(tile_cols, dtype=jnp.int32) * blk_size + blk_at)[None, None, :, None]
    whole_row = tile_row * TB + jnp.arange(TB, dtype=jnp.int32)[None, :, None, None]
    whole_col = tile_col * TB + jnp.arange(TB, dtype=jnp.int32)[None, None, None, :]
    trailing = stiff - update
    result = jnp.where(
        tile_col == 0, row_part[:, :, None, :], jnp.where(tile_row == 0, 0.0, trailing)
    )
    return jnp.where(whole_row >= whole_col, result, 0.0)


def solution(mesh):
    in_specs = (
        P(("blk", "grid"), None),
        P(None, None, ("blk", "grid")),
        P(None, None, ("blk", "grid")),
    )
    out_specs = P(None, "grid", None, "blk")
    return jax.shard_map(shards, mesh=mesh, in_specs=in_specs, out_specs=out_specs, check_vma=False)
```

profile of v0, /device:TPU:1, one launch (start us, length us, event | category | flops | bytes accessed | tf_op | source)
XLA Modules:
  0.0 1185.3 jit_solution(11756267952525601225)
XLA Ops:
  13.7 182.9 %all_gather.13 = f32[81,2048]{0,1:T(8,128)S(1)} all-gather(f32[81,16]{0,1:T(8,128)S(1)} %copy.82), channel_id=1, replica_groups=mesh['blk'=8,'grid'=16] {'blk','grid'}, dimensions={1}, use_global_device_ids=true | all-gather | bytes 668736 | tf_op jit(solution)/shard_map/all_gather | solution.py:146
  197.9 183.5 %all_gather.12 = f32[27,2048]{0,1:T(8,128)} all-gather(f32[27,16]{0,1:T(8,128)S(1)} %reshape.418), channel_id=1, replica_groups=mesh['blk'=8,'grid'=16] {'blk','grid'}, dimensions={1}, use_global_device_ids=true | all-gather | bytes 222912 | tf_op jit(solution)/shard_map/all_gather | solution.py:145
  381.4 184.8 %all_gather.14 = s32[9,2048]{0,1:T(8,128)} all-gather(s32[9,16]{0,1:T(8,128)S(1)} %bitcast.107), channel_id=1, replica_groups=mesh['blk'=8,'grid'=16] {'blk','grid'}, dimensions={1}, use_global_device_ids=true | all-gather | bytes 74304 | tf_op jit(solution)/shard_map/all_gather | solution.py:147
  568.2 172.8 %while.20 = (s32[]{:T(128)}, f32[144,2304]{1,0:T(8,128)}, f32[144]{0:T(256)S(1)}, f32[27,2048]{0,1:T(8,128)}, f32[16,9]{1,0:T(8,128)}, /*index=5*/f32[16,9]{1,0:...) while((s32[]{:T(128)}, f32[144,2304]{1,0:T(8,128)}, ...), condition=%wide.wide.region_2.3_spmd.clone.clone, body=%wide.wide.region_0.2_spmd.sunk.clone.clone.sunk | while | flops 548399360 | bytes 5783860 | solution.py:119
  574.0 2.4 convolution_add_fusion.3
  584.8 2.4 convolution_add_fusion.3
  587.2 1.7 dynamic_update_slice.15
  595.7 2.4 convolution_add_fusion.3
  606.5 2.4 convolution_add_fusion.3
  617.3 2.4 convolution_add_fusion.3
  628.0 2.4 convolution_add_fusion.3
  638.8 2.4 convolution_add_fusion.3
  649.6 2.4 convolution_add_fusion.3
  660.5 2.4 convolution_add_fusion.3
  671.3 2.4 convolution_add_fusion.3
  682.1 2.4 convolution_add_fusion.3
  692.9 2.4 convolution_add_fusion.3
  703.7 2.4 convolution_add_fusion.3
  714.5 2.4 convolution_add_fusion.3
  725.3 2.4 convolution_add_fusion.3
  736.1 2.4 convolution_add_fusion.3
  745.1 10.7 scatter_custom_fusion.1
  759.3 3.3 fusion.33
  764.3 6.0 broadcast_in_dim.83
  770.3 16.2 %scatter_fusion = f32[8,2048,256]{2,0,1:T(8,128)} fusion(f32[8,2048,256]{2,0,1:T(8,128)} %broadcast_in_dim.83, s32[144]{0:T(256)S(1)} %bitcast.113, f32[144,8,256]{2,1,0:T(8,128)S(1)} %bitcast.99), kind=kCustom, calls=%fused_computation | custom fusion | flops 294912 | bytes 3539520 | tf_op jit(solution)/shard_map/scatter-add | solution.py:167
  786.4 15.8 %copy.93 = f32[8,2048,256]{2,1,0:T(8,128)} copy(f32[8,2048,256]{2,0,1:T(8,128)} %scatter_fusion) | data formatting | bytes 33554432 | tf_op jit(solution)/shard_map/scatter-add | solution.py:167
  802.3 18.2 %reshape.386 = f32[128,32768]{1,0:T(8,128)} reshape(f32[8,2048,256]{2,1,0:T(8,128)} %copy.93) | data formatting | bytes 33554432 | tf_op jit(solution)/shard_map/reshape | solution.py:169
  820.6 210.2 %all-reduce.7.cloned.1.call-done = f32[128,32768]{1,0:T(8,128)} async-done(((f32[128,32768]{1,0:T(8,128)}), f32[128,32768]{1,0:T(8,128)}) %all-reduce.7.cloned.1.call-update) | async-done | bytes 16777232
  1033.1 66.6 %all-reduce.5.cloned.1.call-done = f32[1,128,128]{2,1,0:T(8,128)} async-done(((f32[1,128,128]{2,1,0:T(8,128)}), f32[1,128,128]{2,1,0:T(8,128)}) %all-reduce.5.cloned.1.call-update) | async-done | bytes 65552 | tf_op jit(solution)/shard_map/psum | solution.py:18
  1099.9 52.0 %all-gather.2.cloned.1.call-done = f32[16,128,128]{2,1,0:T(8,128)} async-done(((f32[1,128,128]{2,1,0:T(8,128)}), f32[16,128,128]{2,1,0:T(8,128)}) %all-gather.2.cloned.1.call-update) | async-done | bytes 1048592 | tf_op jit(solution)/shard_map/all_gather | solution.py:175
  1153.8 11.7 cholesky.18
  1166.9 9.8 custom-call.6
  (313 shorter events, 158.2 us)
Async XLA Ops:
  6.5 1024.2 %all-reduce.7.cloned.1.call-start = ((), (), s32[]{:S(2)}) async-start(), calls=%async_computation.2 | async-start | bytes 33554432
  12.4 185.4 %copy-start.4 = (f32[1,9,16]{1,2,0:T(8,128)}, f32[1,9,16]{1,2,0:T(8,128)S(1)}, u32[]{:S(2)}) copy-start(f32[1,9,16]{1,2,0:T(8,128)S(1)} %copy.103) | copy-start | bytes 1732
  12.6 185.2 %copy-start.5 = (f32[1,9,16]{1,2,0:T(8,128)}, f32[1,9,16]{1,2,0:T(8,128)S(1)}, u32[]{:S(2)}) copy-start(f32[1,9,16]{1,2,0:T(8,128)S(1)} %copy.102) | copy-start | bytes 1732
  196.6 184.8 %copy-start.3 = (s32[16,9]{1,0:T(8,128)S(1)}, s32[16,9]{1,0:T(8,128)}, u32[]{:S(2)}) copy-start(s32[16,9]{1,0:T(8,128)} %param.7) | copy-start | bytes 1732
  197.8 368.3 %copy-start.1 = (f32[9,9,1]{1,0,2:T(8,128)S(1)}, f32[9,9,1]{1,0,2:T(8,128)}, u32[]{:S(2)}) copy-start(f32[9,9,1]{1,0,2:T(8,128)} %constant.314) | copy-start | bytes 976
  197.8 368.3 %copy-start.2 = (f32[9,9,16]{2,1,0:T(8,128)S(1)}, f32[9,9,16]{2,1,0:T(8,128)}, u32[]{:S(2)}) copy-start(f32[9,9,16]{2,1,0:T(8,128)} %param.8) | copy-start | bytes 15556
  568.2 174.9 %copy-start.9 = (s32[2]{0:T(128)S(1)}, s32[2]{0:T(128)}, u32[]{:S(2)}) copy-start(s32[2]{0:T(128)} %constant.303) | copy-start | bytes 28
  568.2 175.1 %copy-start.8 = (s32[2]{0:T(128)S(1)}, s32[2]{0:T(128)}, u32[]{:S(2)}) copy-start(s32[2]{0:T(128)} %constant.306) | copy-start | bytes 28
  755.8 1.2 copy-start.6
  755.9 1.8 copy-start
  762.6 1.6 copy-start.7
  820.5 279.2 %all-reduce.5.cloned.1.call-start = ((), (), s32[]{:S(2)}) async-start(), calls=%async_computation | async-start | bytes 131072 | tf_op jit(solution)/shard_map/psum | solution.py:18
  1032.8 119.1 %all-gather.2.cloned.1.call-start = ((), (), s32[]{:S(2)}) async-start(), calls=%async_computation.1 | async-start | bytes 1114112 | tf_op jit(solution)/shard_map/all_gather | solution.py:175
  1153.7 23.0 %slice-start = ((f32[16,128,128]{2,1,0:T(8,128)}), f32[15,128,128]{2,1,0:T(8,128)S(1)}, s32[]{:S(2)}) async-start(f32[16,128,128]{2,1,0:T(8,128)} %all-gather.2.cloned.1.call-done), calls=%async_computation.3 | async-start | bytes 1966080 | tf_op jit(solution)/shard_map/slice | solution.py:180
Sparse Core Ops, SparseCore 0:
  820.6 210.1 all-reduce.6
  1033.4 66.3 all-reduce.4
  1102.2 49.6 all-gather.1
where the time goes:
time: 1190 us
  blocking collectives  551 us (46%)
  waiting for transfers between devices  329 us (28%)
  local copies, waits for them, and re-layouts  120 us (10%)
  other arithmetic  99.5 us (8%)
  matrix products  70.7 us (6%)
  between operations  13.4 us (1%)
    unnamed x4, waiting for transfers between devices  210 us
    all_gather x1, blocking collectives, shards(): lax.all_gather(links_flat, ('blk', 'grid'), axis=1, tiled=True)  185 us
    all_gather x1, blocking collectives, shards(): lax.all_gather(points_flat, ('blk', 'grid'), axis=1, tiled=True)  183 us
    all_gather x1, blocking collectives, shards(): lax.all_gather(extract_flat, ('blk', 'grid'), axis=1, tiled=True)  183 us
    psum x1, waiting for transfers between devices, spread(): return lax.psum(jnp.where(mine, array, jnp.zeros_like(array)), axis)  66.6 us
    all_gather x1, waiting for transfers between devices, shards(): panel_tiles = lax.all_gather(mine, 'grid', axis=0, tiled=True)  52 us
    dot_general x16, matrix products, step(): jnp.dot(kernel_block, trial_phi, precision=lax.Precision.HIGHEST, preferr...  38.3 us
    dynamic_update_slice x16, local copies, waits for them, and re-layouts, step(): lax.dynamic_update_slice_in_dim(potential_wide, current + block, offset, 1)  27.4 us
  transfers between devices with their start and end apart: 3, of which 3 were waited for; matrix products, arithmetic and copies ran while one was open for 0% of the time, Pallas kernels for 0%

commit v1 on v0

--- a/solution.py
+++ b/solution.py
@@ -3,6 +3,7 @@
 import jax.numpy as jnp
 from jax import lax
 from jax.sharding import PartitionSpec as P
+from jax.lax import all_gather
 
 M = 2048
 EX = 64
@@ -14,8 +15,12 @@
 
 
 def spread(array, axis, root):
+
+    def keep_up_sheets_here(u, lane_axis):
+        return all_gather(u, lane_axis).sum(axis=0)
+
     mine = lax.axis_index(axis) == root
-    return lax.psum(jnp.where(mine, array, jnp.zeros_like(array)), axis)
+    return keep_up_sheets_here(jnp.where(mine, array, jnp.zeros_like(array)), axis)
 
 
 def bernstein_table():

time: 1190 us -> 1140 us (0.958)
  waiting for transfers between devices: 329 us -> 258 us
  blocking collectives: 551 us -> 574 us
    psum x1 -> x0, waiting for transfers between devices: 66.6 us -> none  [spread(): return lax.psum(jnp.where(mine, array, jnp.zeros_like(array)), axis)]
    all_gather x0 -> x1, blocking collectives: none -> 23.3 us  [keep_up_sheets_here(): return all_gather(u, lane_axis).sum(axis=0)]
    unnamed x4 -> x3, waiting for transfers between devices: 210 us -> 210 us
  transfers between devices with their start and end apart: 3 -> 2, of which waited for: 3 -> 2; matrix products, arithmetic and copies ran while one was open for 0% -> 0% of each run, Pallas kernels for 0% -> 0%
where the time goes in v1:
time: 1140 us
  blocking collectives  574 us (50%)
  waiting for transfers between devices  258 us (23%)
  local copies, waits for them, and re-layouts  120 us (11%)
  other arithmetic  99.2 us (9%)
  matrix products  71.4 us (6%)
  between operations  13.7 us (1%)
    unnamed x3, waiting for transfers between devices  210 us
    all_gather x1, blocking collectives, shards(): lax.all_gather(links_flat, ('blk', 'grid'), axis=1, tiled=True)  185 us
    all_gather x1, blocking collectives, shards(): lax.all_gather(points_flat, ('blk', 'grid'), axis=1, tiled=True)  183 us
    all_gather x1, blocking collectives, shards(): lax.all_gather(extract_flat, ('blk', 'grid'), axis=1, tiled=True)  183 us
    all_gather x1, waiting for transfers between devices, shards(): panel_tiles = lax.all_gather(mine, 'grid', axis=0, tiled=True)  47.8 us
    dot_general x16, matrix products, step(): jnp.dot(kernel_block, trial_phi, precision=lax.Precision.HIGHEST, preferr...  38.3 us
    dynamic_update_slice x16, local copies, waits for them, and re-layouts, step(): lax.dynamic_update_slice_in_dim(potential_wide, current + block, offset, 1)  27.4 us
    dot_general x16, matrix products, step(): jnp.einsum('eka,eaw->ekw', local_values(part_extract), ones, precision=la...  23.8 us
  transfers between devices with their start and end apart: 2, of which 2 were waited for; matrix products, arithmetic and copies ran while one was open for 0% of the time, Pallas kernels for 0%

profile of v1, /device:TPU:1, one launch (start us, length us, event | category | flops | bytes accessed | tf_op | source)
XLA Modules:
  0.0 1139.1 jit_solution(16383727444109570755)
XLA Ops:
  13.7 182.9 %all_gather.17 = f32[81,2048]{0,1:T(8,128)S(1)} all-gather(f32[81,16]{0,1:T(8,128)S(1)} %copy.84), channel_id=1, replica_groups=mesh['blk'=8,'grid'=16] {'blk','grid'}, dimensions={1}, use_global_device_ids=true | all-gather | bytes 668736 | tf_op jit(solution)/shard_map/all_gather | solution.py:151
  197.9 183.5 %all_gather.16 = f32[27,2048]{0,1:T(8,128)} all-gather(f32[27,16]{0,1:T(8,128)S(1)} %reshape.427), channel_id=1, replica_groups=mesh['blk'=8,'grid'=16] {'blk','grid'}, dimensions={1}, use_global_device_ids=true | all-gather | bytes 222912 | tf_op jit(solution)/shard_map/all_gather | solution.py:150
  381.4 184.8 %all_gather.18 = s32[9,2048]{0,1:T(8,128)} all-gather(s32[9,16]{0,1:T(8,128)S(1)} %bitcast.102), channel_id=1, replica_groups=mesh['blk'=8,'grid'=16] {'blk','grid'}, dimensions={1}, use_global_device_ids=true | all-gather | bytes 74304 | tf_op jit(solution)/shard_map/all_gather | solution.py:152
  568.2 172.8 %while.20 = (s32[]{:T(128)}, f32[144,2304]{1,0:T(8,128)}, f32[144]{0:T(256)S(1)}, f32[27,2048]{0,1:T(8,128)}, f32[16,9]{1,0:T(8,128)}, /*index=5*/f32[16,9]{1,0:...) while((s32[]{:T(128)}, f32[144,2304]{1,0:T(8,128)}, ...), condition=%wide.wide.region_2.3_spmd.clone.clone, body=%wide.wide.region_0.2_spmd.sunk.clone.clone.sunk | while | flops 548399360 | bytes 5783860 | solution.py:124
  574.0 2.4 convolution_add_fusion.3
  584.8 2.4 convolution_add_fusion.3
  587.2 1.7 dynamic_update_slice.15
  595.7 2.4 convolution_add_fusion.3
  606.5 2.4 convolution_add_fusion.3
  617.3 2.4 convolution_add_fusion.3
  628.0 2.4 convolution_add_fusion.3
  638.8 2.4 convolution_add_fusion.3
  649.6 2.4 convolution_add_fusion.3
  660.5 2.4 convolution_add_fusion.3
  671.3 2.4 convolution_add_fusion.3
  682.1 2.4 convolution_add_fusion.3
  692.9 2.4 convolution_add_fusion.3
  703.7 2.4 convolution_add_fusion.3
  714.5 2.4 convolution_add_fusion.3
  725.3 2.4 convolution_add_fusion.3
  736.1 2.4 convolution_add_fusion.3
  745.1 10.7 scatter_custom_fusion.1
  759.3 3.3 fusion.34
  764.3 6.0 broadcast_in_dim.83
  770.3 16.2 %scatter_fusion = f32[8,2048,256]{2,0,1:T(8,128)} fusion(f32[8,2048,256]{2,0,1:T(8,128)} %broadcast_in_dim.83, s32[144]{0:T(256)S(1)} %bitcast.108, f32[144,8,256]{2,1,0:T(8,128)S(1)} %bitcast.94), kind=kCustom, calls=%fused_computation | custom fusion | flops 294912 | bytes 3539520 | tf_op jit(solution)/shard_map/scatter-add | solution.py:172
  786.4 15.8 %copy.95 = f32[8,2048,256]{2,1,0:T(8,128)} copy(f32[8,2048,256]{2,0,1:T(8,128)} %scatter_fusion) | data formatting | bytes 33554432 | tf_op jit(solution)/shard_map/scatter-add | solution.py:172
  802.3 18.2 %reshape.388 = f32[128,32768]{1,0:T(8,128)} reshape(f32[8,2048,256]{2,1,0:T(8,128)} %copy.95) | data formatting | bytes 33554432 | tf_op jit(solution)/shard_map/reshape | solution.py:174
  820.6 210.2 %all-reduce.4.cloned.1.call-done = f32[128,32768]{1,0:T(8,128)} async-done(((f32[128,32768]{1,0:T(8,128)}), f32[128,32768]{1,0:T(8,128)}) %all-reduce.4.cloned.1.call-update) | async-done | bytes 16777232
  1032.2 23.3 %all-gather = f32[8,128,1,128]{3,1,2,0:T(8,128)S(1)} all-gather(f32[1,128,1,128]{3,1,2,0:T(8,128)S(1)} %broadcast_select_fusion.3), channel_id=2, replica_groups=mesh['blk'=8,'grid'=16] {'blk'}, dimensions={0}, use_global_device_ids=true | all-gather | bytes 589824 | tf_op jit(solution)/shard_map/all_gather | solution.py:20
  1056.7 47.8 %all-gather.4.cloned.1.call-done = f32[2048,128]{0,1:T(8,128)} async-done(((f32[128,128]{0,1:T(8,128)}), f32[2048,128]{0,1:T(8,128)}) %all-gather.4.cloned.1.call-update) | async-done | bytes 1048592 | tf_op jit(solution)/shard_map/all_gather | solution.py:180
  1106.5 11.7 %cholesky.18 = f32[128,128]{1,0:T(8,128)S(1)} custom-call(f32[128,128]{1,0:T(8,128)S(1)} %fusion.23), custom_call_target="Cholesky" | custom-call | tf_op jit(solution)/shard_map/jit(cholesky)/cholesky | solution.py:183
  1119.6 9.8 custom-call.6
  (314 shorter events, 159.3 us)
Async XLA Ops:
  6.5 1024.2 %all-reduce.4.cloned.1.call-start = ((), (), s32[]{:S(2)}) async-start(), calls=%async_computation.1 | async-start | bytes 33554432
  12.4 185.4 %copy-start.5 = (f32[1,9,16]{1,2,0:T(8,128)}, f32[1,9,16]{1,2,0:T(8,128)S(1)}, u32[]{:S(2)}) copy-start(f32[1,9,16]{1,2,0:T(8,128)S(1)} %copy.107) | copy-start | bytes 1732
  12.6 185.2 %copy-start.6 = (f32[1,9,16]{1,2,0:T(8,128)}, f32[1,9,16]{1,2,0:T(8,128)S(1)}, u32[]{:S(2)}) copy-start(f32[1,9,16]{1,2,0:T(8,128)S(1)} %copy.106) | copy-start | bytes 1732
  196.6 184.8 %copy-start.4 = (s32[16,9]{1,0:T(8,128)S(1)}, s32[16,9]{1,0:T(8,128)}, u32[]{:S(2)}) copy-start(s32[16,9]{1,0:T(8,128)} %param.7) | copy-start | bytes 1732
  197.8 368.3 %copy-start.2 = (f32[9,9,1]{1,0,2:T(8,128)S(1)}, f32[9,9,1]{1,0,2:T(8,128)}, u32[]{:S(2)}) copy-start(f32[9,9,1]{1,0,2:T(8,128)} %constant.314) | copy-start | bytes 976
  197.8 368.3 %copy-start.3 = (f32[9,9,16]{2,1,0:T(8,128)S(1)}, f32[9,9,16]{2,1,0:T(8,128)}, u32[]{:S(2)}) copy-start(f32[9,9,16]{2,1,0:T(8,128)} %param.8) | copy-start | bytes 15556
  568.2 174.9 %copy-start.10 = (s32[2]{0:T(128)S(1)}, s32[2]{0:T(128)}, u32[]{:S(2)}) copy-start(s32[2]{0:T(128)} %constant.303) | copy-start | bytes 28
  568.2 175.1 %copy-start.9 = (s32[2]{0:T(128)S(1)}, s32[2]{0:T(128)}, u32[]{:S(2)}) copy-start(s32[2]{0:T(128)} %constant.306) | copy-start | bytes 28
  755.8 1.2 copy-start.7
  755.9 1.8 copy-start
  762.6 1.6 copy-start.8
  820.5 284.0 %all-gather.4.cloned.1.call-start = ((), (), s32[]{:S(2)}) async-start(), calls=%async_computation | async-start | bytes 1114112 | tf_op jit(solution)/shard_map/all_gather | solution.py:180
  1104.5 24.9 %copy-start.1 = (f32[2048,128]{0,1:T(8,128)S(1)}, f32[2048,128]{0,1:T(8,128)}, u32[]{:S(2)}) copy-start(f32[2048,128]{0,1:T(8,128)} %all-gather.4.cloned.1.call-done) | copy-start | bytes 3145732
Sparse Core Ops, SparseCore 0:
  820.6 210.1 all-reduce.3
  1056.7 47.7 all-gather.3
